TPU v7x, 256 devices: a whole 4x4x8 slice. The times are simulated.
256 devices in a mesh: blk: 8 (over x_hi, y), group: 32 (over z, x_lo, core).
Axes of the slice: x: 4 (x_hi: 2, x_lo: 2; x = x_hi * 2 + x_lo), y: 4, z: 8, core: 2. Of those that a mesh axis runs over, the one named last changes fastest.
Arguments:
- walk_rows: bfloat16 [4096, 131072], P('blk', 'group'), may hold values from -6 to 6
- col_values: bfloat16 [49152, 4096], P('group', 'blk'), may hold values from -0.02734375 to 0.02734375
- col_index: int32 [96, 8], P('group'), may hold values from 0 to 7
- col_count: int32 [32, 8], P('group'), may hold values from 1 to 3, as said below
Outputs:
- inflated: float32 [4096, 4096], P(('blk', 'group'))
Inputs may be any that keep to these rules, and one draw needn't show every extreme that they name: `col_count`: each list holds 1 to 3 valid slots; some list holds 3; contents of the other slots are arbitrary.
All inputs are finite; a program needn't handle non-finite values.
Results may differ from a plain program's by a relative error of at most 0.0003.
Values may be sent and summed in bfloat16 or wider, within the bound.
No kernel may reach another device: no remote copies, remote signals or barrier semaphores. Data moves between devices by JAX's collectives and lax.ppermute only.
A program may use at most 64 MiB of HBM per device.

v0:
```python
import jax
import jax.numpy as jnp
from jax import lax
from jax.sharding import PartitionSpec as P


def shifted(shard, axis, by):
    size = lax.axis_size(axis)
    return lax.ppermute(shard, axis, [(i, (i + by) % size) for i in range(size)])


def on_device(walk_rows, col_values, col_index, col_count):
    width = col_values.shape[1]
    slots = col_values.shape[0] // width
    nblock = lax.axis_size("blk")
    myself = lax.axis_index("blk")
    rows_here = walk_rows.shape[0]
    share = rows_here // lax.axis_size("group")

    def panel_product(rows, values, panel):
        index = lax.dynamic_slice_in_dim(col_index, panel, 1, 1)[:, 0]
        count = lax.dynamic_slice_in_dim(col_count, panel, 1, 1)[0, 0]
        total = jnp.zeros((rows.shape[0], width), jnp.float32)
        for slot in range(slots):
            block = lax.dynamic_slice_in_dim(rows, index[slot] * width, width, 1)
            piece = values[slot * width : (slot + 1) * width]
            product = jnp.dot(block, piece, preferred_element_type=jnp.float32)
            total = total + jnp.where(slot < count, product, jnp.zeros_like(product))
        return total

    def turn(step, carry):
        values, result = carry
        panel = (myself - step) % nblock
        part = panel_product(walk_rows, values, panel)
        reduced = lax.psum_scatter(part, "group", scatter_dimension=0, tiled=True)
        result = lax.dynamic_update_slice_in_dim(result, reduced, panel * width, 1)
        values = shifted(values, "blk", 1)
        return (values, result)

    start_out = jnp.zeros((share, nblock * width), jnp.float32)
    unused, expanded = lax.fori_loop(0, nblock, turn, (col_values, start_out))
    squared = expanded * expanded
    column = jnp.sum(squared, axis=0)
    total = lax.psum(column, ("blk", "group"))
    scale = total / (nblock * rows_here) + 1e-06
    return squared / scale


def solution(mesh):
    return jax.shard_map(
        on_device,
        mesh=mesh,
        in_specs=(P("blk", "group"), P("group", "blk"), P("group", None), P("group", None)),
        out_specs=P(("blk", "group"), None),
        check_vma=False,
    )
```

profile of v0, /device:TPU:1, one launch (start us, length us, event | category | flops | bytes accessed | tf_op | source)
XLA Modules:
  0.0 1125.3 jit_solution(7067308069750690020)
XLA Ops:
  6.6 1.4 copy-done
  7.9 1030.1 %while.17 = (s32[]{:T(128)}, bf16[1536,512]{1,0:T(8,128)(2,1)S(1)}, f32[16,4096]{1,0:T(8,128)S(1)}, s32[]{:T(128)}, s32[1,8]{1,0:T(1,128)S(1)}, /*index=5*/s32[3...) while((s32[]{:T(128)}, bf16[1536,512]{1,0:T(8,128)(2,1)S(1)}, ...), condition=%wide.region_2.3_spmd, body=%wide.region_0.2_spmd.sunk | while | flops 806617088 | bytes 21137560 | solution.py:41
  10.5 0.7 fusion.29
  12.4 2.1 convolution_select_fusion.5
  14.5 1.5 convolution_select_fusion.6
  16.0 2.5 fusion.30
  18.5 2.2 collective-permute-start
  20.7 117.8 %reduce-scatter.2.cloned.1.call-done = f32[16,512]{1,0:T(8,128)} async-done(((f32[512,512]{1,0:T(8,128)}), f32[16,512]{1,0:T(8,128)}) %reduce-scatter.2.cloned.1.call-update) | async-done | bytes 32784 | tf_op jit(solution)/shard_map/while/body/eval_jaxpr/reduce_scatter | solution.py:35
  138.5 0.8 constant_dynamic-update-slice_fusion.2
  143.7 2.1 convolution_select_fusion.5
  145.8 1.5 convolution_select_fusion.6
  147.3 2.5 fusion.30
  149.9 117.1 %reduce-scatter.2.cloned.1.call-done = f32[16,512]{1,0:T(8,128)} async-done(((f32[512,512]{1,0:T(8,128)}), f32[16,512]{1,0:T(8,128)}) %reduce-scatter.2.cloned.1.call-update) | async-done | bytes 32784 | tf_op jit(solution)/shard_map/while/body/eval_jaxpr/reduce_scatter | solution.py:35
  267.0 0.8 constant_dynamic-update-slice_fusion.2
  272.2 2.1 convolution_select_fusion.5
  274.3 1.5 convolution_select_fusion.6
  275.8 2.5 fusion.30
  278.4 116.7 %reduce-scatter.2.cloned.1.call-done = f32[16,512]{1,0:T(8,128)} async-done(((f32[512,512]{1,0:T(8,128)}), f32[16,512]{1,0:T(8,128)}) %reduce-scatter.2.cloned.1.call-update) | async-done | bytes 32784 | tf_op jit(solution)/shard_map/while/body/eval_jaxpr/reduce_scatter | solution.py:35
  395.1 0.8 constant_dynamic-update-slice_fusion.2
  400.4 2.1 convolution_select_fusion.5
  402.5 1.5 convolution_select_fusion.6
  404.0 2.5 fusion.30
  406.6 116.8 %reduce-scatter.2.cloned.1.call-done = f32[16,512]{1,0:T(8,128)} async-done(((f32[512,512]{1,0:T(8,128)}), f32[16,512]{1,0:T(8,128)}) %reduce-scatter.2.cloned.1.call-update) | async-done | bytes 32784 | tf_op jit(solution)/shard_map/while/body/eval_jaxpr/reduce_scatter | solution.py:35
  523.4 0.8 constant_dynamic-update-slice_fusion.2
  526.8 0.7 fusion.29
  528.7 2.1 convolution_select_fusion.5
  530.8 1.5 convolution_select_fusion.6
  532.3 2.5 fusion.30
  535.0 116.8 %reduce-scatter.2.cloned.1.call-done = f32[16,512]{1,0:T(8,128)} async-done(((f32[512,512]{1,0:T(8,128)}), f32[16,512]{1,0:T(8,128)}) %reduce-scatter.2.cloned.1.call-update) | async-done | bytes 32784 | tf_op jit(solution)/shard_map/while/body/eval_jaxpr/reduce_scatter | solution.py:35
  651.9 0.8 constant_dynamic-update-slice_fusion.2
  657.1 2.1 convolution_select_fusion.5
  659.2 1.5 convolution_select_fusion.6
  660.7 2.5 fusion.30
  663.5 116.9 %reduce-scatter.2.cloned.1.call-done = f32[16,512]{1,0:T(8,128)} async-done(((f32[512,512]{1,0:T(8,128)}), f32[16,512]{1,0:T(8,128)}) %reduce-scatter.2.cloned.1.call-update) | async-done | bytes 32784 | tf_op jit(solution)/shard_map/while/body/eval_jaxpr/reduce_scatter | solution.py:35
  780.3 0.8 constant_dynamic-update-slice_fusion.2
  785.6 2.1 convolution_select_fusion.5
  787.7 1.5 convolution_select_fusion.6
  789.2 2.5 fusion.30
  791.9 116.9 %reduce-scatter.2.cloned.1.call-done = f32[16,512]{1,0:T(8,128)} async-done(((f32[512,512]{1,0:T(8,128)}), f32[16,512]{1,0:T(8,128)}) %reduce-scatter.2.cloned.1.call-update) | async-done | bytes 32784 | tf_op jit(solution)/shard_map/while/body/eval_jaxpr/reduce_scatter | solution.py:35
  908.8 0.8 constant_dynamic-update-slice_fusion.2
  912.1 0.7 fusion.29
  914.0 2.1 convolution_select_fusion.5
  916.1 1.5 convolution_select_fusion.6
  917.6 2.5 fusion.30
  920.6 116.6 %reduce-scatter.2.cloned.1.call-done = f32[16,512]{1,0:T(8,128)} async-done(((f32[512,512]{1,0:T(8,128)}), f32[16,512]{1,0:T(8,128)}) %reduce-scatter.2.cloned.1.call-update) | async-done | bytes 32784 | tf_op jit(solution)/shard_map/while/body/eval_jaxpr/reduce_scatter | solution.py:35
  1037.3 0.8 constant_dynamic-update-slice_fusion.2
  1038.1 79.7 %psum.7 = f32[4096]{0:T(1024)S(1)} all-reduce(f32[4096]{0:T(1024)S(1)} %multiply_reduce_fusion), channel_id=1, replica_groups=mesh['blk'=8,'group'=32] {'blk','group'}, use_global_device_ids=true, to_apply=%region_4.5 | all-reduce | flops 4096 | bytes 32768 | tf_op jit(solution)/shard_map/psum | solution.py:44
  1117.7 0.7 multiply_divide_fusion
  (68 shorter events, 11.2 us)
Async XLA Ops:
  6.5 1.4 copy-start
  6.5 1.4 copy-start.1
  6.5 1.4 copy-start.2
  7.9 130.5 %reduce-scatter.2.cloned.1.call-start = ((), (), s32[]{:S(2)}) async-start(), calls=%async_computation.1 | async-start | bytes 1081344 | tf_op jit(solution)/shard_map/while/body/eval_jaxpr/reduce_scatter | solution.py:35
  18.5 120.8 %collective-permute-start = (bf16[1536,512]{1,0:T(8,128)(2,1)S(1)}, bf16[1536,512]{1,0:T(8,128)(2,1)S(1)}, u32[]{:S(2)}, u32[]{:S(2)}) collective-permute-start(bf16[1536,512]{1,0:T(8,128)(2,1)S(1)} %copy.10), channel_id=1, source_target_pairs={{0,32},{32,64},{64,96},{96,128},{128,160},{160,192},{192,224},{224... | collective-permute-start | bytes 4718600 | tf_op jit(solution)/shard_map/while/body/eval_jaxpr/ppermute | solution.py:9
  139.3 127.7 %reduce-scatter.2.cloned.1.call-start = ((), (), s32[]{:S(2)}) async-start(), calls=%async_computation.1 | async-start | bytes 1081344 | tf_op jit(solution)/shard_map/while/body/eval_jaxpr/reduce_scatter | solution.py:35
  149.8 117.9 %collective-permute-start = (bf16[1536,512]{1,0:T(8,128)(2,1)S(1)}, bf16[1536,512]{1,0:T(8,128)(2,1)S(1)}, u32[]{:S(2)}, u32[]{:S(2)}) collective-permute-start(bf16[1536,512]{1,0:T(8,128)(2,1)S(1)} %copy.10), channel_id=1, source_target_pairs={{0,32},{32,64},{64,96},{96,128},{128,160},{160,192},{192,224},{224... | collective-permute-start | bytes 4718600 | tf_op jit(solution)/shard_map/while/body/eval_jaxpr/ppermute | solution.py:9
  267.7 127.4 %reduce-scatter.2.cloned.1.call-start = ((), (), s32[]{:S(2)}) async-start(), calls=%async_computation.1 | async-start | bytes 1081344 | tf_op jit(solution)/shard_map/while/body/eval_jaxpr/reduce_scatter | solution.py:35
  278.3 117.6 %collective-permute-start = (bf16[1536,512]{1,0:T(8,128)(2,1)S(1)}, bf16[1536,512]{1,0:T(8,128)(2,1)S(1)}, u32[]{:S(2)}, u32[]{:S(2)}) collective-permute-start(bf16[1536,512]{1,0:T(8,128)(2,1)S(1)} %copy.10), channel_id=1, source_target_pairs={{0,32},{32,64},{64,96},{96,128},{128,160},{160,192},{192,224},{224... | collective-permute-start | bytes 4718600 | tf_op jit(solution)/shard_map/while/body/eval_jaxpr/ppermute | solution.py:9
  395.9 127.5 %reduce-scatter.2.cloned.1.call-start = ((), (), s32[]{:S(2)}) async-start(), calls=%async_computation.1 | async-start | bytes 1081344 | tf_op jit(solution)/shard_map/while/body/eval_jaxpr/reduce_scatter | solution.py:35
  406.4 117.8 %collective-permute-start = (bf16[1536,512]{1,0:T(8,128)(2,1)S(1)}, bf16[1536,512]{1,0:T(8,128)(2,1)S(1)}, u32[]{:S(2)}, u32[]{:S(2)}) collective-permute-start(bf16[1536,512]{1,0:T(8,128)(2,1)S(1)} %copy.10), channel_id=1, source_target_pairs={{0,32},{32,64},{64,96},{96,128},{128,160},{160,192},{192,224},{224... | collective-permute-start | bytes 4718600 | tf_op jit(solution)/shard_map/while/body/eval_jaxpr/ppermute | solution.py:9
  524.2 127.7 %reduce-scatter.2.cloned.1.call-start = ((), (), s32[]{:S(2)}) async-start(), calls=%async_computation.1 | async-start | bytes 1081344 | tf_op jit(solution)/shard_map/while/body/eval_jaxpr/reduce_scatter | solution.py:35
  534.8 117.9 %collective-permute-start = (bf16[1536,512]{1,0:T(8,128)(2,1)S(1)}, bf16[1536,512]{1,0:T(8,128)(2,1)S(1)}, u32[]{:S(2)}, u32[]{:S(2)}) collective-permute-start(bf16[1536,512]{1,0:T(8,128)(2,1)S(1)} %copy.10), channel_id=1, source_target_pairs={{0,32},{32,64},{64,96},{96,128},{128,160},{160,192},{192,224},{224... | collective-permute-start | bytes 4718600 | tf_op jit(solution)/shard_map/while/body/eval_jaxpr/ppermute | solution.py:9
  652.6 127.7 %reduce-scatter.2.cloned.1.call-start = ((), (), s32[]{:S(2)}) async-start(), calls=%async_computation.1 | async-start | bytes 1081344 | tf_op jit(solution)/shard_map/while/body/eval_jaxpr/reduce_scatter | solution.py:35
  663.2 117.9 %collective-permute-start = (bf16[1536,512]{1,0:T(8,128)(2,1)S(1)}, bf16[1536,512]{1,0:T(8,128)(2,1)S(1)}, u32[]{:S(2)}, u32[]{:S(2)}) collective-permute-start(bf16[1536,512]{1,0:T(8,128)(2,1)S(1)} %copy.10), channel_id=1, source_target_pairs={{0,32},{32,64},{64,96},{96,128},{128,160},{160,192},{192,224},{224... | collective-permute-start | bytes 4718600 | tf_op jit(solution)/shard_map/while/body/eval_jaxpr/ppermute | solution.py:9
  781.1 127.7 %reduce-scatter.2.cloned.1.call-start = ((), (), s32[]{:S(2)}) async-start(), calls=%async_computation.1 | async-start | bytes 1081344 | tf_op jit(solution)/shard_map/while/body/eval_jaxpr/reduce_scatter | solution.py:35
  791.7 117.9 %collective-permute-start = (bf16[1536,512]{1,0:T(8,128)(2,1)S(1)}, bf16[1536,512]{1,0:T(8,128)(2,1)S(1)}, u32[]{:S(2)}, u32[]{:S(2)}) collective-permute-start(bf16[1536,512]{1,0:T(8,128)(2,1)S(1)} %copy.10), channel_id=1, source_target_pairs={{0,32},{32,64},{64,96},{96,128},{128,160},{160,192},{192,224},{224... | collective-permute-start | bytes 4718600 | tf_op jit(solution)/shard_map/while/body/eval_jaxpr/ppermute | solution.py:9
  909.6 127.7 %reduce-scatter.2.cloned.1.call-start = ((), (), s32[]{:S(2)}) async-start(), calls=%async_computation.1 | async-start | bytes 1081344 | tf_op jit(solution)/shard_map/while/body/eval_jaxpr/reduce_scatter | solution.py:35
  920.1 117.9 %collective-permute-start = (bf16[1536,512]{1,0:T(8,128)(2,1)S(1)}, bf16[1536,512]{1,0:T(8,128)(2,1)S(1)}, u32[]{:S(2)}, u32[]{:S(2)}) collective-permute-start(bf16[1536,512]{1,0:T(8,128)(2,1)S(1)} %copy.10), channel_id=1, source_target_pairs={{0,32},{32,64},{64,96},{96,128},{128,160},{160,192},{192,224},{224... | collective-permute-start | bytes 4718600 | tf_op jit(solution)/shard_map/while/body/eval_jaxpr/ppermute | solution.py:9
Sparse Core Ops, SparseCore 0:
  18.6 119.8 reduce-scatter.1
  149.9 116.9 reduce-scatter.1
  278.4 116.6 reduce-scatter.1
  406.6 116.8 reduce-scatter.1
  534.9 116.9 reduce-scatter.1
  663.3 116.9 reduce-scatter.1
  791.8 116.9 reduce-scatter.1
  920.2 116.9 reduce-scatter.1
where the time goes:
time: 1130 us
  waiting for transfers between devices  936 us (83%)
  blocking collectives  79.7 us (7%)
  matrix products  48.4 us (4%)
  loops' own time  24.6 us (2%)
  local copies, waits for them, and re-layouts  13.6 us (1%)
  between operations  13.4 us (1%)
    reduce_scatter x8, waiting for transfers between devices, turn(): reduced = lax.psum_scatter(part, 'group', scatter_dimension=0, tiled=True)  936 us
    psum x1, blocking collectives, on_device(): total = lax.psum(column, ('blk', 'group'))  79.7 us
    dot_general x24, matrix products, panel_product(): product = jnp.dot(block, piece, preferred_element_type=jnp.float32)  48.4 us
    another operation x1, loops' own time, on_device(): unused, expanded = lax.fori_loop(0, nblock, turn, (col_values, start_out))  24.6 us
  transfers between devices with their start and end apart: 16, of which 8 were waited for; matrix products, arithmetic and copies ran while one was open for 1% of the time, Pallas kernels for 0%

commit v1 on v0

--- a/solution.py
+++ b/solution.py
@@ -41,7 +41,7 @@
     unused, expanded = lax.fori_loop(0, nblock, turn, (col_values, start_out))
     squared = expanded * expanded
     column = jnp.sum(squared, axis=0)
-    total = lax.psum(column, ("blk", "group"))
+    total = lax.psum(lax.psum(column, "group"), "blk")
     scale = total / (nblock * rows_here) + 1e-06
     return squared / scale
 

time: 1130 us -> 1190 us (1.053)
  blocking collectives: 79.7 us -> 139 us
    psum x1 -> x2, blocking collectives: 79.7 us -> 139 us  [on_device(): total = lax.psum(lax.psum(column, 'group'), 'blk')]
where the time goes in v1:
time: 1190 us; the launch traced here: 1180 us
  waiting for transfers between devices  935 us (79%)
  blocking collectives  139 us (12%)
  matrix products  48 us (4%)
  loops' own time  25.2 us (2%)
  local copies, waits for them, and re-layouts  13.6 us (1%)
  between operations  13.4 us (1%)
    reduce_scatter x8, waiting for transfers between devices, turn(): reduced = lax.psum_scatter(part, 'group', scatter_dimension=0, tiled=True)  935 us
    psum x2, blocking collectives, on_device(): total = lax.psum(lax.psum(column, 'group'), 'blk')  139 us
    dot_general x24, matrix products, panel_product(): product = jnp.dot(block, piece, preferred_element_type=jnp.float32)  48 us
    another operation x1, loops' own time, on_device(): unused, expanded = lax.fori_loop(0, nblock, turn, (col_values, start_out))  25.2 us
  transfers between devices with their start and end apart: 16, of which 8 were waited for; matrix products, arithmetic and copies ran while one was open for 1% of the time, Pallas kernels for 0%

profile of v1, /device:TPU:1, one launch (start us, length us, event | category | flops | bytes accessed | tf_op | source)
XLA Modules:
  0.0 1183.7 jit_solution(3891503458169299501)
XLA Ops:
  6.6 1.4 copy-done
  7.9 1029.5 %while.17 = (s32[]{:T(128)}, bf16[1536,512]{1,0:T(8,128)(2,1)S(1)}, f32[16,4096]{1,0:T(8,128)S(1)}, s32[]{:T(128)}, s32[1,8]{1,0:T(1,128)S(1)}, /*index=5*/s32[3...) while((s32[]{:T(128)}, bf16[1536,512]{1,0:T(8,128)(2,1)S(1)}, ...), condition=%wide.region_2.3_spmd, body=%wide.region_0.2_spmd.sunk | while | flops 806617088 | bytes 21137560 | solution.py:41
  12.4 2.0 convolution_select_fusion.5
  14.5 1.5 convolution_select_fusion.6
  16.0 2.5 fusion.30
  18.5 2.2 collective-permute-start
  20.7 117.8 %reduce-scatter.2.cloned.1.call-done = f32[16,512]{1,0:T(8,128)} async-done(((f32[512,512]{1,0:T(8,128)}), f32[16,512]{1,0:T(8,128)}) %reduce-scatter.2.cloned.1.call-update) | async-done | bytes 32784 | tf_op jit(solution)/shard_map/while/body/eval_jaxpr/reduce_scatter | solution.py:35
  138.5 0.8 constant_dynamic-update-slice_fusion.2
  141.8 0.6 fusion.29
  143.7 2.0 convolution_select_fusion.5
  145.8 1.5 convolution_select_fusion.6
  147.3 2.5 fusion.30
  149.9 117.0 %reduce-scatter.2.cloned.1.call-done = f32[16,512]{1,0:T(8,128)} async-done(((f32[512,512]{1,0:T(8,128)}), f32[16,512]{1,0:T(8,128)}) %reduce-scatter.2.cloned.1.call-update) | async-done | bytes 32784 | tf_op jit(solution)/shard_map/while/body/eval_jaxpr/reduce_scatter | solution.py:35
  266.9 0.8 constant_dynamic-update-slice_fusion.2
  270.2 0.6 fusion.29
  272.2 2.0 convolution_select_fusion.5
  274.2 1.5 convolution_select_fusion.6
  275.7 2.5 fusion.30
  278.3 117.0 %reduce-scatter.2.cloned.1.call-done = f32[16,512]{1,0:T(8,128)} async-done(((f32[512,512]{1,0:T(8,128)}), f32[16,512]{1,0:T(8,128)}) %reduce-scatter.2.cloned.1.call-update) | async-done | bytes 32784 | tf_op jit(solution)/shard_map/while/body/eval_jaxpr/reduce_scatter | solution.py:35
  395.3 0.8 constant_dynamic-update-slice_fusion.2
  400.6 2.0 convolution_select_fusion.5
  402.6 1.5 convolution_select_fusion.6
  404.1 2.5 fusion.30
  406.7 116.7 %reduce-scatter.2.cloned.1.call-done = f32[16,512]{1,0:T(8,128)} async-done(((f32[512,512]{1,0:T(8,128)}), f32[16,512]{1,0:T(8,128)}) %reduce-scatter.2.cloned.1.call-update) | async-done | bytes 32784 | tf_op jit(solution)/shard_map/while/body/eval_jaxpr/reduce_scatter | solution.py:35
  523.4 0.8 constant_dynamic-update-slice_fusion.2
  528.7 2.0 convolution_select_fusion.5
  530.7 1.5 convolution_select_fusion.6
  532.2 2.5 fusion.30
  535.0 116.8 %reduce-scatter.2.cloned.1.call-done = f32[16,512]{1,0:T(8,128)} async-done(((f32[512,512]{1,0:T(8,128)}), f32[16,512]{1,0:T(8,128)}) %reduce-scatter.2.cloned.1.call-update) | async-done | bytes 32784 | tf_op jit(solution)/shard_map/while/body/eval_jaxpr/reduce_scatter | solution.py:35
  651.8 0.8 constant_dynamic-update-slice_fusion.2
  657.0 2.0 convolution_select_fusion.5
  659.1 1.5 convolution_select_fusion.6
  660.6 2.5 fusion.30
  663.3 117.0 %reduce-scatter.2.cloned.1.call-done = f32[16,512]{1,0:T(8,128)} async-done(((f32[512,512]{1,0:T(8,128)}), f32[16,512]{1,0:T(8,128)}) %reduce-scatter.2.cloned.1.call-update) | async-done | bytes 32784 | tf_op jit(solution)/shard_map/while/body/eval_jaxpr/reduce_scatter | solution.py:35
  780.3 0.8 constant_dynamic-update-slice_fusion.2
  785.6 2.0 convolution_select_fusion.5
  787.6 1.5 convolution_select_fusion.6
  789.1 2.5 fusion.30
  792.0 116.5 %reduce-scatter.2.cloned.1.call-done = f32[16,512]{1,0:T(8,128)} async-done(((f32[512,512]{1,0:T(8,128)}), f32[16,512]{1,0:T(8,128)}) %reduce-scatter.2.cloned.1.call-update) | async-done | bytes 32784 | tf_op jit(solution)/shard_map/while/body/eval_jaxpr/reduce_scatter | solution.py:35
  908.5 0.8 constant_dynamic-update-slice_fusion.2
  913.8 2.0 convolution_select_fusion.5
  915.8 1.5 convolution_select_fusion.6
  917.3 2.5 fusion.30
  920.2 116.5 %reduce-scatter.2.cloned.1.call-done = f32[16,512]{1,0:T(8,128)} async-done(((f32[512,512]{1,0:T(8,128)}), f32[16,512]{1,0:T(8,128)}) %reduce-scatter.2.cloned.1.call-update) | async-done | bytes 32784 | tf_op jit(solution)/shard_map/while/body/eval_jaxpr/reduce_scatter | solution.py:35
  1036.7 0.8 constant_dynamic-update-slice_fusion.2
  1037.5 104.4 %psum.14 = f32[4096]{0:T(1024)S(1)} all-reduce(f32[4096]{0:T(1024)S(1)} %multiply_reduce_fusion), channel_id=1, replica_groups=mesh['blk'=8,'group'=32] {'group'}, use_global_device_ids=true, to_apply=%region_4.5 | all-reduce | flops 4096 | bytes 32768 | tf_op jit(solution)/shard_map/psum | solution.py:44
  1141.9 34.3 %psum.15 = f32[4096]{0:T(1024)S(1)} all-reduce(f32[4096]{0:T(1024)S(1)} %psum.14), channel_id=1, replica_groups=mesh['blk'=8,'group'=32] {'blk'}, use_global_device_ids=true, to_apply=%region_5.6 | all-reduce | flops 4096 | bytes 32768 | tf_op jit(solution)/shard_map/psum | solution.py:44
  1176.2 0.7 multiply_divide_fusion
  (69 shorter events, 11.6 us)
Async XLA Ops:
  6.5 1.4 copy-start
  6.5 1.4 copy-start.1
  6.5 1.4 copy-start.2
  7.9 130.5 %reduce-scatter.2.cloned.1.call-start = ((), (), s32[]{:S(2)}) async-start(), calls=%async_computation.1 | async-start | bytes 1081344 | tf_op jit(solution)/shard_map/while/body/eval_jaxpr/reduce_scatter | solution.py:35
  18.5 120.8 %collective-permute-start = (bf16[1536,512]{1,0:T(8,128)(2,1)S(1)}, bf16[1536,512]{1,0:T(8,128)(2,1)S(1)}, u32[]{:S(2)}, u32[]{:S(2)}) collective-permute-start(bf16[1536,512]{1,0:T(8,128)(2,1)S(1)} %copy.10), channel_id=1, source_target_pairs={{0,32},{32,64},{64,96},{96,128},{128,160},{160,192},{192,224},{224... | collective-permute-start | bytes 4718600 | tf_op jit(solution)/shard_map/while/body/eval_jaxpr/ppermute | solution.py:9
  139.2 127.7 %reduce-scatter.2.cloned.1.call-start = ((), (), s32[]{:S(2)}) async-start(), calls=%async_computation.1 | async-start | bytes 1081344 | tf_op jit(solution)/shard_map/while/body/eval_jaxpr/reduce_scatter | solution.py:35
  149.8 117.9 %collective-permute-start = (bf16[1536,512]{1,0:T(8,128)(2,1)S(1)}, bf16[1536,512]{1,0:T(8,128)(2,1)S(1)}, u32[]{:S(2)}, u32[]{:S(2)}) collective-permute-start(bf16[1536,512]{1,0:T(8,128)(2,1)S(1)} %copy.10), channel_id=1, source_target_pairs={{0,32},{32,64},{64,96},{96,128},{128,160},{160,192},{192,224},{224... | collective-permute-start | bytes 4718600 | tf_op jit(solution)/shard_map/while/body/eval_jaxpr/ppermute | solution.py:9
  267.7 127.7 %reduce-scatter.2.cloned.1.call-start = ((), (), s32[]{:S(2)}) async-start(), calls=%async_computation.1 | async-start | bytes 1081344 | tf_op jit(solution)/shard_map/while/body/eval_jaxpr/reduce_scatter | solution.py:35
  278.2 117.9 %collective-permute-start = (bf16[1536,512]{1,0:T(8,128)(2,1)S(1)}, bf16[1536,512]{1,0:T(8,128)(2,1)S(1)}, u32[]{:S(2)}, u32[]{:S(2)}) collective-permute-start(bf16[1536,512]{1,0:T(8,128)(2,1)S(1)} %copy.10), channel_id=1, source_target_pairs={{0,32},{32,64},{64,96},{96,128},{128,160},{160,192},{192,224},{224... | collective-permute-start | bytes 4718600 | tf_op jit(solution)/shard_map/while/body/eval_jaxpr/ppermute | solution.py:9
  396.1 127.3 %reduce-scatter.2.cloned.1.call-start = ((), (), s32[]{:S(2)}) async-start(), calls=%async_computation.1 | async-start | bytes 1081344 | tf_op jit(solution)/shard_map/while/body/eval_jaxpr/reduce_scatter | solution.py:35
  406.6 117.6 %collective-permute-start = (bf16[1536,512]{1,0:T(8,128)(2,1)S(1)}, bf16[1536,512]{1,0:T(8,128)(2,1)S(1)}, u32[]{:S(2)}, u32[]{:S(2)}) collective-permute-start(bf16[1536,512]{1,0:T(8,128)(2,1)S(1)} %copy.10), channel_id=1, source_target_pairs={{0,32},{32,64},{64,96},{96,128},{128,160},{160,192},{192,224},{224... | collective-permute-start | bytes 4718600 | tf_op jit(solution)/shard_map/while/body/eval_jaxpr/ppermute | solution.py:9
  524.2 127.6 %reduce-scatter.2.cloned.1.call-start = ((), (), s32[]{:S(2)}) async-start(), calls=%async_computation.1 | async-start | bytes 1081344 | tf_op jit(solution)/shard_map/while/body/eval_jaxpr/reduce_scatter | solution.py:35
  534.7 117.8 %collective-permute-start = (bf16[1536,512]{1,0:T(8,128)(2,1)S(1)}, bf16[1536,512]{1,0:T(8,128)(2,1)S(1)}, u32[]{:S(2)}, u32[]{:S(2)}) collective-permute-start(bf16[1536,512]{1,0:T(8,128)(2,1)S(1)} %copy.10), channel_id=1, source_target_pairs={{0,32},{32,64},{64,96},{96,128},{128,160},{160,192},{192,224},{224... | collective-permute-start | bytes 4718600 | tf_op jit(solution)/shard_map/while/body/eval_jaxpr/ppermute | solution.py:9
  652.5 127.7 %reduce-scatter.2.cloned.1.call-start = ((), (), s32[]{:S(2)}) async-start(), calls=%async_computation.1 | async-start | bytes 1081344 | tf_op jit(solution)/shard_map/while/body/eval_jaxpr/reduce_scatter | solution.py:35
  663.1 118.0 %collective-permute-start = (bf16[1536,512]{1,0:T(8,128)(2,1)S(1)}, bf16[1536,512]{1,0:T(8,128)(2,1)S(1)}, u32[]{:S(2)}, u32[]{:S(2)}) collective-permute-start(bf16[1536,512]{1,0:T(8,128)(2,1)S(1)} %copy.10), channel_id=1, source_target_pairs={{0,32},{32,64},{64,96},{96,128},{128,160},{160,192},{192,224},{224... | collective-permute-start | bytes 4718600 | tf_op jit(solution)/shard_map/while/body/eval_jaxpr/ppermute | solution.py:9
  781.1 127.5 %reduce-scatter.2.cloned.1.call-start = ((), (), s32[]{:S(2)}) async-start(), calls=%async_computation.1 | async-start | bytes 1081344 | tf_op jit(solution)/shard_map/while/body/eval_jaxpr/reduce_scatter | solution.py:35
  791.6 117.7 %collective-permute-start = (bf16[1536,512]{1,0:T(8,128)(2,1)S(1)}, bf16[1536,512]{1,0:T(8,128)(2,1)S(1)}, u32[]{:S(2)}, u32[]{:S(2)}) collective-permute-start(bf16[1536,512]{1,0:T(8,128)(2,1)S(1)} %copy.10), channel_id=1, source_target_pairs={{0,32},{32,64},{64,96},{96,128},{128,160},{160,192},{192,224},{224... | collective-permute-start | bytes 4718600 | tf_op jit(solution)/shard_map/while/body/eval_jaxpr/ppermute | solution.py:9
  909.3 127.4 %reduce-scatter.2.cloned.1.call-start = ((), (), s32[]{:S(2)}) async-start(), calls=%async_computation.1 | async-start | bytes 1081344 | tf_op jit(solution)/shard_map/while/body/eval_jaxpr/reduce_scatter | solution.py:35
  919.8 117.6 %collective-permute-start = (bf16[1536,512]{1,0:T(8,128)(2,1)S(1)}, bf16[1536,512]{1,0:T(8,128)(2,1)S(1)}, u32[]{:S(2)}, u32[]{:S(2)}) collective-permute-start(bf16[1536,512]{1,0:T(8,128)(2,1)S(1)} %copy.10), channel_id=1, source_target_pairs={{0,32},{32,64},{64,96},{96,128},{128,160},{160,192},{192,224},{224... | collective-permute-start | bytes 4718600 | tf_op jit(solution)/shard_map/while/body/eval_jaxpr/ppermute | solution.py:9
Sparse Core Ops, SparseCore 0:
  18.6 119.8 reduce-scatter.1
  149.9 116.9 reduce-scatter.1
  278.3 116.9 reduce-scatter.1
  406.7 116.6 reduce-scatter.1
  534.8 116.9 reduce-scatter.1
  663.2 117.0 reduce-scatter.1
  791.7 116.7 reduce-scatter.1
  919.9 116.6 reduce-scatter.1
